TPU v7x, 256 devices: a whole 4x4x8 slice. The times are simulated.
256 devices in a mesh: cplx: 4 (over y_hi, core), row: 64 (over z, x, y_lo).
Axes of the slice: x: 4, y: 4 (y_hi: 2, y_lo: 2; y = y_hi * 2 + y_lo), z: 8, core: 2. Of those that a mesh axis runs over, the one named last changes fastest.
Arguments:
- pair_state: bfloat16 [2048, 512, 128], P(('cplx', 'row')), parts along dimension 0, may hold values from -60 to 60
- cotangent: bfloat16 [2048, 512, 128], P(('cplx', 'row')), parts along dimension 0, may hold values from -6 to 6
- token_mask: int32 [2048], P('cplx'), parts along dimension 0, may hold values 0 or 1
- input_gain: float32 [128], replicated, may hold values from 0.25 to 1.75
- input_bias: float32 [128], replicated, may hold values from -3 to 3
- input_weight: bfloat16 [128, 640], replicated, may hold values from -0.5 to 0.5
- output_gain: float32 [128], replicated, may hold values from 0.25 to 1.75
- output_bias: float32 [128], replicated, may hold values from -3 to 3
- output_weight: bfloat16 [128, 128], replicated, may hold values from -0.5 to 0.5
Outputs:
- pair_gradient: bfloat16 [2048, 512, 128], P(('cplx', 'row')), parts along dimension 0
- input_gradient: float32 [512, 640], P(('cplx', 'row')), parts along dimension 0
- output_gradient: float32 [512, 128], P(('cplx', 'row')), parts along dimension 0
There are 4 independent parts, one for each index of `cplx`. A program takes and returns all parts, laid end to end along the dimension named above; an argument that names none is the same for every part. Nothing has to cross between parts.
Inputs may be any that keep to these rules, and one draw needn't show every extreme that they name: `token_mask`: 1 marks a token of the complex, 0 a padding slot.
All inputs are finite; a program needn't handle non-finite values.
Results may differ from a plain program's by a relative error of at most 0.0076.
Values may be sent and summed in bfloat16 or wider, within the bound.
No kernel may reach another device: no remote copies, remote signals or barrier semaphores. Data moves between devices by JAX's collectives and lax.ppermute only.
A program may use at most 64 MiB of HBM per device.

v0:
```python
import jax
import jax.numpy as jnp
from jax import lax
from jax.sharding import PartitionSpec as P

epsilon = 1e-05


def norm_parts(values, norm_axis):
    average = jnp.mean(values, axis=norm_axis, keepdims=True)
    centered = values - average
    variance = jnp.mean(centered * centered, axis=norm_axis, keepdims=True)
    inverse = lax.rsqrt(variance + epsilon)
    return (centered * inverse, inverse)


def norm_backward(upstream, scaled, inverse, norm_axis):
    first_mean = jnp.mean(upstream, axis=norm_axis, keepdims=True)
    second = jnp.mean(upstream * scaled, axis=norm_axis, keepdims=True)
    return inverse * (upstream - first_mean - scaled * second)


def to_pieces(values, slab_count):
    return values.reshape(
        slab_count, values.shape[0] // slab_count, values.shape[1], values.shape[2]
    )


def from_pieces(values):
    return values.reshape(values.shape[0] * values.shape[1], values.shape[2], values.shape[3])


def triangle(left_slab, right_slab):
    result = jnp.einsum(
        "xcik,xcjk->xcij", left_slab, right_slab, preferred_element_type=jnp.float32
    )
    return result.astype(jnp.bfloat16)


def factor_gradients(grad_slab, left_slab, right_slab):
    left_part = jnp.einsum(
        "xcij,xcjk->xcik", grad_slab, right_slab, preferred_element_type=jnp.float32
    )
    right_part = jnp.einsum(
        "xcij,xcik->xcjk", grad_slab, left_slab, preferred_element_type=jnp.float32
    )
    return (left_part.astype(jnp.bfloat16), right_part.astype(jnp.bfloat16))


def project(normed, weight_block):
    return jnp.einsum("rnd,de->ern", normed, weight_block, preferred_element_type=jnp.float32)


def on_device(
    pair_state,
    cotangent,
    token_mask,
    input_gain,
    input_bias,
    input_weight,
    output_gain,
    output_bias,
    output_weight,
):
    row_count = pair_state.shape[0]
    tokens = pair_state.shape[1]
    channels = pair_state.shape[2]
    slab_count = lax.axis_size("row")
    token_float = token_mask.astype(jnp.float32)
    row_start = lax.axis_index("row") * row_count
    row_float = lax.dynamic_slice_in_dim(token_float, row_start, row_count)
    pair_mask = (row_float[:, None] * token_float[None, :])[None]
    scaled_in, inverse_in = norm_parts(pair_state.astype(jnp.float32), 2)
    normed = (scaled_in * input_gain + input_bias).astype(jnp.bfloat16)
    left_proj = project(normed, input_weight[:, 0 : 2 * channels])
    right_proj = project(normed, input_weight[:, 2 * channels : 4 * channels])
    out_gate = jax.nn.sigmoid(project(normed, input_weight[:, 4 * channels :]))
    left_lin = left_proj[:channels]
    left_gate = jax.nn.sigmoid(left_proj[channels:])
    right_lin = right_proj[:channels]
    right_gate = jax.nn.sigmoid(right_proj[channels:])
    left_rows = to_pieces((pair_mask * left_gate * left_lin).astype(jnp.bfloat16), slab_count)
    right_rows = to_pieces((pair_mask * right_gate * right_lin).astype(jnp.bfloat16), slab_count)
    left_slab, right_slab = (
        lax.all_to_all(left_rows, "row", split_axis=0, concat_axis=2, tiled=True),
        lax.all_to_all(right_rows, "row", split_axis=0, concat_axis=2, tiled=True),
    )
    product_slab = triangle(left_slab, right_slab)
    product_pieces = lax.all_to_all(product_slab, "row", split_axis=2, concat_axis=0, tiled=True)
    product_rows = from_pieces(product_pieces).astype(jnp.float32)
    scaled_out, inverse_out = norm_parts(product_rows, 0)
    normed_out = (scaled_out * output_gain[:, None, None] + output_bias[:, None, None]).astype(
        jnp.bfloat16
    )
    projected = jnp.einsum(
        "crn,cd->drn", normed_out, output_weight, preferred_element_type=jnp.float32
    )
    upstream = jnp.transpose(cotangent, (2, 0, 1)).astype(jnp.float32)
    mixed_grad = (upstream * out_gate).astype(jnp.bfloat16)
    gate_grad = upstream * projected * out_gate * (1.0 - out_gate)
    out_norm_grad = jnp.einsum(
        "drn,cd->crn", mixed_grad, output_weight, preferred_element_type=jnp.float32
    )
    product_grad = norm_backward(
        out_norm_grad * output_gain[:, None, None], scaled_out, inverse_out, 0
    ).astype(jnp.bfloat16)
    grad_rows = to_pieces(product_grad, slab_count)
    grad_slab = lax.all_to_all(grad_rows, "row", split_axis=0, concat_axis=2, tiled=True)
    left_part, right_part = factor_gradients(grad_slab, left_slab, right_slab)
    left_pieces, right_pieces = (
        lax.all_to_all(left_part, "row", split_axis=2, concat_axis=0, tiled=True),
        lax.all_to_all(right_part, "row", split_axis=2, concat_axis=0, tiled=True),
    )
    left_back = from_pieces(left_pieces).astype(jnp.float32) * pair_mask
    right_back = from_pieces(right_pieces).astype(jnp.float32) * pair_mask
    proj_grad = jnp.concatenate(
        [
            (left_back * left_gate).astype(jnp.bfloat16),
            (left_back * left_lin * left_gate * (1.0 - left_gate)).astype(jnp.bfloat16),
            (right_back * right_gate).astype(jnp.bfloat16),
            (right_back * right_lin * right_gate * (1.0 - right_gate)).astype(jnp.bfloat16),
            gate_grad.astype(jnp.bfloat16),
        ],
        axis=0,
    )
    normed_grad = jnp.einsum(
        "ern,de->rnd", proj_grad, input_weight, preferred_element_type=jnp.float32
    )
    pair_gradient = norm_backward(normed_grad * input_gain, scaled_in, inverse_in, 2).astype(
        jnp.bfloat16
    )
    input_term = (
        jnp.einsum("rnd,ern->de", normed, proj_grad, preferred_element_type=jnp.float32) / tokens
    )
    output_term = (
        jnp.einsum("crn,drn->cd", normed_out, mixed_grad, preferred_element_type=jnp.float32)
        / tokens
    )
    input_gradient, output_gradient = (
        lax.psum_scatter(input_term, "row", scatter_dimension=0, tiled=True),
        lax.psum_scatter(output_term, "row", scatter_dimension=0, tiled=True),
    )
    return (pair_gradient, input_gradient, output_gradient)


def solution(mesh):
    return jax.shard_map(
        on_device,
        mesh=mesh,
        in_specs=(
            P(("cplx", "row"), None, None),
            P(("cplx", "row"), None, None),
            P("cplx"),
            P(),
            P(),
            P(),
            P(),
            P(),
            P(),
        ),
        out_specs=(
            P(("cplx", "row"), None, None),
            P(("cplx", "row"), None),
            P(("cplx", "row"), None),
        ),
        check_vma=False,
    )
```

profile of v0, /device:TPU:16, one launch (start us, length us, event | category | flops | bytes accessed | tf_op | source)
XLA Modules:
  0.0 879.4 jit_solution(5712075969375751696)
XLA Ops:
  7.2 1.6 copy.29
  9.3 2.7 convolution_bitcast_fusion
  12.1 2.8 convolution_bitcast_fusion.1
  15.0 4.7 multiply_convert_fusion.5
  19.7 1.2 reshape.130
  21.0 3.4 copy.32
  24.4 12.9 %all-to-all-start = ((bf16[64,2,8,512]{3,1,2,0:T(2,128)(2,1)}), bf16[64,2,8,512]{3,1,2,0:T(2,128)(2,1)}, u32[]{:S(2)}, u32[]{:S(2)}) async-start(bf16[64,2,8,512]{3,1,2,0:T(2,128)(2,1)} %copy.32), calls=%async_computation | async-start | bytes 2097152 | tf_op jit(solution)/shard_map/all_to_all | solution.py:85
  37.8 1.1 copy.36
  38.9 27.1 %all-to-all-done = bf16[64,2,8,512]{3,1,2,0:T(2,128)(2,1)} async-done(((bf16[64,2,8,512]{3,1,2,0:T(2,128)(2,1)}), bf16[64,2,8,512]{3,1,2,0:T(2,128)(2,1)}, u32[]{:S(2)}, u32[]{:S(2)}) %all-to-all-start) | async-done | bytes 1048608 | tf_op jit(solution)/shard_map/all_to_all | solution.py:85
  66.0 34.1 %all_to_all.72 = bf16[64,2,8,512]{3,1,2,0:T(2,128)(2,1)S(1)} all-to-all(bf16[64,2,8,512]{3,1,2,0:T(2,128)(2,1)S(1)} %copy.36), channel_id=1, replica_groups=mesh['cplx'=4,'row'=64] {'row'}, dimensions={0} | all-to-all | bytes 2097152 | tf_op jit(solution)/shard_map/all_to_all | solution.py:86
  100.1 1.0 copy-done.9
  101.1 2.0 fusion.27
  103.1 2.0 copy.38
  105.2 5.8 all-to-all-start.2
  111.0 1.3 copy.40
  112.3 2.3 add_divide_fusion
  114.6 24.3 %all-to-all-done.2 = bf16[1,2,512,512]{3,1,0,2:T(2,128)(2,1)S(1)} async-done(((bf16[1,2,512,512]{3,1,0,2:T(2,128)(2,1)}), bf16[1,2,512,512]{3,1,0,2:T(2,128)(2,1)S(1)}, u32[]{:S(2)}, u32[]{:S(2)}) %all-to-all-start.2) | async-done | bytes 1048608 | tf_op jit(solution)/shard_map/all_to_all | solution.py:89
  138.9 2.1 copy_bitcast_fusion.2
  141.8 2.7 reshape.136
  144.6 2.6 multiply_reduce_fusion
  147.2 2.7 bitcast_reduce_fusion
  149.9 1.7 fusion.23
  151.5 2.2 reshape.134
  153.8 2.4 copy.43
  156.2 33.4 %all_to_all.73 = bf16[64,2,8,512]{3,1,2,0:T(2,128)(2,1)S(1)} all-to-all(bf16[64,2,8,512]{3,1,2,0:T(2,128)(2,1)S(1)} %copy.43), channel_id=1, replica_groups=mesh['cplx'=4,'row'=64] {'row'}, dimensions={0} | all-to-all | bytes 2097152 | tf_op jit(solution)/shard_map/all_to_all | solution.py:108
  190.6 2.0 fusion.29
  192.5 2.1 copy.48
  194.6 6.2 all-to-all-start.5
  200.9 2.3 fusion.28
  203.1 2.0 copy.45
  205.2 23.1 %all-to-all-done.5 = bf16[1,2,512,512]{3,1,0,2:T(2,128)(2,1)} async-done(((bf16[1,2,512,512]{3,1,0,2:T(2,128)(2,1)}), bf16[1,2,512,512]{3,1,0,2:T(2,128)(2,1)}, u32[]{:S(2)}, u32[]{:S(2)}) %all-to-all-start.5) | async-done | bytes 1048608 | tf_op jit(solution)/shard_map/all_to_all | solution.py:112
  228.3 6.0 all-to-all-start.4
  235.7 3.1 fusion.31
  238.8 3.3 copy_bitcast_fusion
  242.1 3.7 reshape.138
  245.8 16.2 %all-to-all-done.4 = bf16[1,2,512,512]{3,1,0,2:T(2,128)(2,1)} async-done(((bf16[1,2,512,512]{3,1,0,2:T(2,128)(2,1)}), bf16[1,2,512,512]{3,1,0,2:T(2,128)(2,1)}, u32[]{:S(2)}, u32[]{:S(2)}) %all-to-all-start.4) | async-done | bytes 1048608 | tf_op jit(solution)/shard_map/all_to_all | solution.py:111
  262.0 3.3 copy_bitcast_fusion.1
  265.3 3.6 reshape.137
  269.0 3.0 fusion.32
  272.4 2.6 fusion.33
  279.3 2.3 copy-done.7
  281.6 2.5 fusion.30
  284.1 3.5 multiply_reduce_fusion.1
  287.7 1.6 fusion.10
  289.2 2.3 copy.51
  291.5 578.5 %all-reduce.5.cloned.1.call-done = (f32[128,640]{1,0:T(8,128)}, f32[128,128]{1,0:T(8,128)}) async-done(((f32[128,640]{1,0:T(8,128)}, f32[128,128]{1,0:T(8,128)}), (f32[128,640]{1,0:T(8,128)}, f32[128,128]{1,0:T(8,128)})) %all-reduce.5.cloned.1.call-update) | async-done | bytes 393232
  870.0 1.3 constant_dynamic-slice_fusion.1
  871.3 1.2 constant_dynamic-slice_fusion
  (54 shorter events, 8.2 us)
Async XLA Ops:
  7.2 140.0 %copy-start = (bf16[128,128]{1,0:T(8,128)(2,1)S(1)}, bf16[128,128]{1,0:T(8,128)(2,1)}, u32[]{:S(2)}) copy-start(bf16[128,128]{1,0:T(8,128)(2,1)} %param.17) | copy-start | bytes 98308
  7.2 2.1 copy-start.12
  7.2 2.1 copy-start.14
  7.2 2.1 copy-start.11
  12.1 2.8 copy-start.15
  24.4 41.6 %all-to-all-start = ((bf16[64,2,8,512]{3,1,2,0:T(2,128)(2,1)}), bf16[64,2,8,512]{3,1,2,0:T(2,128)(2,1)}, u32[]{:S(2)}, u32[]{:S(2)}) async-start(bf16[64,2,8,512]{3,1,2,0:T(2,128)(2,1)} %copy.32), calls=%async_computation | async-start | bytes 2097152 | tf_op jit(solution)/shard_map/all_to_all | solution.py:85
  100.1 1.0 copy-start.9
  103.1 7.9 copy-start.8
  105.2 33.7 %all-to-all-start.2 = ((bf16[1,2,512,512]{3,1,0,2:T(2,128)(2,1)}), bf16[1,2,512,512]{3,1,0,2:T(2,128)(2,1)S(1)}, u32[]{:S(2)}, u32[]{:S(2)}) async-start(bf16[1,2,512,512]{3,1,0,2:T(2,128)(2,1)} %copy.38), calls=%async_computation.2 | async-start | bytes 2097152 | tf_op jit(solution)/shard_map/all_to_all | solution.py:89
  138.9 2.1 copy-start.5
  141.8 5.4 copy-start.13
  189.6 1.0 copy-start.10
  194.6 33.7 %all-to-all-start.5 = ((bf16[1,2,512,512]{3,1,0,2:T(2,128)(2,1)}), bf16[1,2,512,512]{3,1,0,2:T(2,128)(2,1)}, u32[]{:S(2)}, u32[]{:S(2)}) async-start(bf16[1,2,512,512]{3,1,0,2:T(2,128)(2,1)} %copy.48), calls=%async_computation.5 | async-start | bytes 2097152 | tf_op jit(solution)/shard_map/all_to_all | solution.py:112
  203.1 31.3 %copy-start.17 = (u32[256]{0:T(256)S(1)}, u32[256]{0:T(256)}, u32[]{:S(2)}) copy-start(u32[256]{0:T(256)} %constant.37) | copy-start | bytes 3076
  203.1 32.5 %copy-start.16 = (f32[128]{0:T(128)S(1)}, f32[128]{0:T(128)}, u32[]{:S(2)}) copy-start(f32[128]{0:T(128)} %param.16) | copy-start | bytes 1540
  228.3 33.7 %all-to-all-start.4 = ((bf16[1,2,512,512]{3,1,0,2:T(2,128)(2,1)}), bf16[1,2,512,512]{3,1,0,2:T(2,128)(2,1)}, u32[]{:S(2)}, u32[]{:S(2)}) async-start(bf16[1,2,512,512]{3,1,0,2:T(2,128)(2,1)} %copy.45), calls=%async_computation.4 | async-start | bytes 2097152 | tf_op jit(solution)/shard_map/all_to_all | solution.py:111
  234.4 635.6 %all-reduce.5.cloned.1.call-start = ((), (), s32[]{:S(2)}) async-start(), calls=%async_computation.6 | async-start | bytes 786432
  269.0 3.4 copy-start.2
  272.4 2.8 copy-start.1
  272.4 3.5 copy-start.3
  276.6 1.6 copy-start.4
  276.6 1.8 copy-start.6
  279.3 2.3 copy-start.7
Sparse Core Ops, SparseCore 0:
  287.8 582.1 all-reduce.4
where the time goes:
time: 880 us; the launch traced here: 879 us
  waiting for transfers between devices  669 us (76%)
  blocking collectives  67.5 us (8%)
  local copies, waits for them, and re-layouts  41.9 us (5%)
  starting transfers between devices  31.1 us (4%)
  other arithmetic  27.9 us (3%)
  matrix products  26.7 us (3%)
  between operations  15.1 us (2%)
    unnamed x2, waiting for transfers between devices  578 us
    all_to_all x1, blocking collectives, on_device(): lax.all_to_all(right_rows, 'row', split_axis=0, concat_axis=2, tiled=True)  34.1 us
    all_to_all x1, blocking collectives, on_device(): lax.all_to_all(grad_rows, 'row', split_axis=0, concat_axis=2, tiled=True)  33.4 us
    all_to_all x1, waiting for transfers between devices, on_device(): lax.all_to_all(left_rows, 'row', split_axis=0, concat_axis=2, tiled=True)  27.1 us
    all_to_all x1, waiting for transfers between devices, on_device(): lax.all_to_all(product_slab, 'row', split_axis=2, concat_axis=0, tiled=True)  24.3 us
    all_to_all x1, waiting for transfers between devices, on_device(): lax.all_to_all(right_part, 'row', split_axis=2, concat_axis=0, tiled=True)  23.1 us
  transfers between devices with their start and end apart: 5, of which 5 were waited for; matrix products, arithmetic and copies ran while one was open for 3% of the time, Pallas kernels for 0%

commit v1 on v0

--- a/solution.py
+++ b/solution.py
@@ -81,8 +81,21 @@
     right_gate = jax.nn.sigmoid(right_proj[channels:])
     left_rows = to_pieces((pair_mask * left_gate * left_lin).astype(jnp.bfloat16), slab_count)
     right_rows = to_pieces((pair_mask * right_gate * right_lin).astype(jnp.bfloat16), slab_count)
+
+    def _tell_forms(xin):
+        next_value = jnp.concatenate(
+            lax.all_to_all(
+                jnp.stack(jnp.split(xin, lax.axis_size("row"), axis=0)),
+                "row",
+                split_axis=0,
+                concat_axis=0,
+            ),
+            axis=2,
+        )
+        return next_value
+
     left_slab, right_slab = (
-        lax.all_to_all(left_rows, "row", split_axis=0, concat_axis=2, tiled=True),
+        _tell_forms(left_rows),
         lax.all_to_all(right_rows, "row", split_axis=0, concat_axis=2, tiled=True),
     )
     product_slab = triangle(left_slab, right_slab)

time: 880 us -> 922 us (1.048)
  local copies, waits for them, and re-layouts: 41.9 us -> 72.7 us
    unnamed x42 -> x101, local copies, waits for them, and re-layouts: 14.9 us -> 49.6 us
    all_to_all x1, waiting for transfers between devices: 23.1 us -> 8.82 us  [on_device(): lax.all_to_all(right_part, 'row', split_axis=2, concat_axis=0, tiled=True)]
where the time goes in v1:
time: 922 us; the launch traced here: 913 us
  waiting for transfers between devices  662 us (72%)
  local copies, waits for them, and re-layouts  72.7 us (8%)
  blocking collectives  67.5 us (7%)
  other arithmetic  34.7 us (4%)
  starting transfers between devices  31 us (3%)
  matrix products  29.1 us (3%)
  between operations  15.4 us (2%)
    unnamed x2, waiting for transfers between devices  578 us
    unnamed x101, local copies, waits for them, and re-layouts  49.6 us
    all_to_all x1, blocking collectives, on_device(): lax.all_to_all(right_rows, 'row', split_axis=0, concat_axis=2, tiled=True)  34.1 us
    all_to_all x1, blocking collectives, on_device(): lax.all_to_all(grad_rows, 'row', split_axis=0, concat_axis=2, tiled=True)  33.4 us
    all_to_all x1, waiting for transfers between devices, _tell_forms(): lax.all_to_all(jnp.stack(jnp.split(xin, lax.axis_size('row'), axis=0)), '...  27.1 us
    all_to_all x1, waiting for transfers between devices, on_device(): lax.all_to_all(product_slab, 'row', split_axis=2, concat_axis=0, tiled=True)  24.5 us
    all_to_all x1, waiting for transfers between devices, on_device(): lax.all_to_all(left_part, 'row', split_axis=2, concat_axis=0, tiled=True)  23.3 us
  transfers between devices with their start and end apart: 5, of which 5 were waited for; matrix products, arithmetic and copies ran while one was open for 3% of the time, Pallas kernels for 0%

profile of v1, /device:TPU:16, one launch (start us, length us, event | category | flops | bytes accessed | tf_op | source)
XLA Modules:
  0.0 912.6 jit_solution(17831221057615042887)
XLA Ops:
  7.2 1.6 copy.30
  9.3 2.8 convolution_bitcast_fusion
  12.1 2.9 convolution_bitcast_fusion.1
  15.1 4.7 multiply_convert_fusion.4
  59.8 12.9 %all-to-all-start = ((bf16[64,1,2,8,512]{4,2,3,1,0:T(2,128)(2,1)}), bf16[64,1,2,8,512]{4,2,3,1,0:T(2,128)(2,1)}, u32[]{:S(2)}, u32[]{:S(2)}) async-start(bf16[64,1,2,8,512]{4,2,3,1,0:T(2,128)(2,1)} %constant_dynamic-update-slice_fusion), calls=%async_computation | async-start | bytes 2097152 | tf_op jit(solution)/shard_map/all_to_all | solution.py:87
  73.1 1.1 copy.35
  74.3 27.1 %all-to-all-done = bf16[64,1,2,8,512]{4,2,3,1,0:T(2,128)(2,1)} async-done(((bf16[64,1,2,8,512]{4,2,3,1,0:T(2,128)(2,1)}), bf16[64,1,2,8,512]{4,2,3,1,0:T(2,128)(2,1)}, u32[]{:S(2)}, u32[]{:S(2)}) %all-to-all-start) | async-done | bytes 1048608 | tf_op jit(solution)/shard_map/all_to_all | solution.py:87
  101.4 34.1 %all_to_all.62 = bf16[64,2,8,512]{3,1,2,0:T(2,128)(2,1)S(1)} all-to-all(bf16[64,2,8,512]{3,1,2,0:T(2,128)(2,1)S(1)} %copy.35), channel_id=1, replica_groups=mesh['cplx'=4,'row'=64] {'row'}, dimensions={0} | all-to-all | bytes 2097152 | tf_op jit(solution)/shard_map/all_to_all | solution.py:99
  135.5 1.0 copy-done.6
  136.4 2.0 fusion.27
  138.4 2.0 copy.38
  140.5 5.8 all-to-all-start.2
  146.3 1.3 copy.40
  147.7 2.2 add_divide_fusion
  149.9 24.5 %all-to-all-done.2 = bf16[1,2,512,512]{3,1,0,2:T(2,128)(2,1)S(1)} async-done(((bf16[1,2,512,512]{3,1,0,2:T(2,128)(2,1)}), bf16[1,2,512,512]{3,1,0,2:T(2,128)(2,1)S(1)}, u32[]{:S(2)}, u32[]{:S(2)}) %all-to-all-start.2) | async-done | bytes 1048608 | tf_op jit(solution)/shard_map/all_to_all | solution.py:102
  175.2 2.1 copy_bitcast_fusion.2
  177.3 1.4 multiply_reduce_fusion
  178.8 2.7 reshape.266
  181.5 2.7 bitcast_reduce_fusion
  184.2 1.7 fusion.23
  185.8 2.2 reshape.264
  188.1 2.5 copy.43
  190.5 33.4 %all_to_all.63 = bf16[64,2,8,512]{3,1,2,0:T(2,128)(2,1)S(1)} all-to-all(bf16[64,2,8,512]{3,1,2,0:T(2,128)(2,1)S(1)} %copy.43), channel_id=1, replica_groups=mesh['cplx'=4,'row'=64] {'row'}, dimensions={0} | all-to-all | bytes 2097152 | tf_op jit(solution)/shard_map/all_to_all | solution.py:121
  224.0 1.0 copy-done.8
  225.7 2.0 copy.45
  227.7 6.2 all-to-all-start.4
  234.0 2.3 fusion.29
  236.3 2.1 copy.49
  238.4 23.3 %all-to-all-done.4 = bf16[1,2,512,512]{3,1,0,2:T(2,128)(2,1)} async-done(((bf16[1,2,512,512]{3,1,0,2:T(2,128)(2,1)}), bf16[1,2,512,512]{3,1,0,2:T(2,128)(2,1)}, u32[]{:S(2)}, u32[]{:S(2)}) %all-to-all-start.4) | async-done | bytes 1048608 | tf_op jit(solution)/shard_map/all_to_all | solution.py:124
  261.7 6.0 all-to-all-start.5
  269.0 3.1 fusion.31
  272.1 3.3 copy_bitcast_fusion.1
  275.5 3.7 reshape.267
  279.1 4.0 fusion.32
  283.1 3.4 fusion.33
  286.5 8.8 all-to-all-done.5
  295.3 3.4 copy_bitcast_fusion
  298.8 3.6 reshape.268
  302.4 4.1 fusion.34
  306.5 3.6 fusion.35
  310.1 1.9 fusion.26
  312.0 3.5 multiply_reduce_fusion.1
  315.5 5.0 fusion.30
  320.5 1.6 fusion.10
  322.1 2.3 copy.52
  324.4 578.5 %all-reduce.5.cloned.1.call-done = (f32[128,640]{1,0:T(8,128)}, f32[128,128]{1,0:T(8,128)}) async-done(((f32[128,640]{1,0:T(8,128)}, f32[128,128]{1,0:T(8,128)}), (f32[128,640]{1,0:T(8,128)}, f32[128,128]{1,0:T(8,128)})) %all-reduce.5.cloned.1.call-update) | async-done | bytes 393232
  902.8 1.3 constant_dynamic-slice_fusion.1
  904.2 1.2 constant_dynamic-slice_fusion
  (112 shorter events, 43.2 us)
Async XLA Ops:
  7.2 174.3 %copy-start = (bf16[128,128]{1,0:T(8,128)(2,1)S(1)}, bf16[128,128]{1,0:T(8,128)(2,1)}, u32[]{:S(2)}) copy-start(bf16[128,128]{1,0:T(8,128)(2,1)} %param.17) | copy-start | bytes 98308
  7.2 2.1 copy-start.9
  7.2 2.1 copy-start.10
  7.2 2.1 copy-start.12
  12.1 2.9 copy-start.13
  59.8 41.6 %all-to-all-start = ((bf16[64,1,2,8,512]{4,2,3,1,0:T(2,128)(2,1)}), bf16[64,1,2,8,512]{4,2,3,1,0:T(2,128)(2,1)}, u32[]{:S(2)}, u32[]{:S(2)}) async-start(bf16[64,1,2,8,512]{4,2,3,1,0:T(2,128)(2,1)} %constant_dynamic-update-slice_fusion), calls=%async_computation | async-start | bytes 2097152 | tf_op jit(solution)/shard_map/all_to_all | solution.py:87
  135.5 1.0 copy-start.6
  138.4 7.9 copy-start.5
  140.5 33.9 %all-to-all-start.2 = ((bf16[1,2,512,512]{3,1,0,2:T(2,128)(2,1)}), bf16[1,2,512,512]{3,1,0,2:T(2,128)(2,1)S(1)}, u32[]{:S(2)}, u32[]{:S(2)}) async-start(bf16[1,2,512,512]{3,1,0,2:T(2,128)(2,1)} %copy.38), calls=%async_computation.2 | async-start | bytes 2097152 | tf_op jit(solution)/shard_map/all_to_all | solution.py:102
  178.7 2.7 copy-start.11
  188.1 36.9 %copy-start.7 = (bf16[64,2,8,512]{3,1,2,0:T(2,128)(2,1)S(1)}, bf16[64,2,8,512]{3,1,2,0:T(2,128)(2,1)}, u32[]{:S(2)}) copy-start(bf16[64,2,8,512]{3,1,2,0:T(2,128)(2,1)} %copy-done.6) | copy-start | bytes 3145732
  224.0 1.0 copy-start.8
  227.7 33.9 %all-to-all-start.4 = ((bf16[1,2,512,512]{3,1,0,2:T(2,128)(2,1)}), bf16[1,2,512,512]{3,1,0,2:T(2,128)(2,1)}, u32[]{:S(2)}, u32[]{:S(2)}) async-start(bf16[1,2,512,512]{3,1,0,2:T(2,128)(2,1)} %copy.45), calls=%async_computation.4 | async-start | bytes 2097152 | tf_op jit(solution)/shard_map/all_to_all | solution.py:124
  236.3 31.5 %copy-start.15 = (u32[256]{0:T(256)S(1)}, u32[256]{0:T(256)}, u32[]{:S(2)}) copy-start(u32[256]{0:T(256)} %constant.37) | copy-start | bytes 3076
  236.3 32.7 %copy-start.14 = (f32[128]{0:T(128)S(1)}, f32[128]{0:T(128)}, u32[]{:S(2)}) copy-start(f32[128]{0:T(128)} %param.16) | copy-start | bytes 1540
  261.7 33.7 %all-to-all-start.5 = ((bf16[1,2,512,512]{3,1,0,2:T(2,128)(2,1)}), bf16[1,2,512,512]{3,1,0,2:T(2,128)(2,1)}, u32[]{:S(2)}, u32[]{:S(2)}) async-start(bf16[1,2,512,512]{3,1,0,2:T(2,128)(2,1)} %copy.49), calls=%async_computation.5 | async-start | bytes 2097152 | tf_op jit(solution)/shard_map/all_to_all | solution.py:125
  267.7 635.1 %all-reduce.5.cloned.1.call-start = ((), (), s32[]{:S(2)}) async-start(), calls=%async_computation.6 | async-start | bytes 786432
  279.1 4.0 copy-start.2
  302.4 4.1 copy-start.1
  306.5 3.6 copy-start.3
  306.5 3.6 copy-start.4
Sparse Core Ops, SparseCore 0:
  320.6 582.1 all-reduce.4
